TPU v7x, 32 devices: a whole 2x2x4 slice. The times are simulated.
32 devices in a mesh: shard: 4 (over y, x), ctx: 2 (over core), tp: 4 (over z).
Axes of the slice: x: 2, y: 2, z: 4, core: 2. Of those that a mesh axis runs over, the one named last changes fastest.
Arguments:
- tokens: bfloat16 [4, 1024, 1536], P('shard', ('ctx', 'tp')), may hold values from -6 to 6
- cotangent: bfloat16 [4, 1024, 1536], P('shard', ('ctx', 'tp')), may hold values from -6 to 6
- lengths: int32 [4], P('shard'), may hold values from 256 to 1024, as said below
- w_qkv: bfloat16 [1536, 3, 1536], P(('shard', 'ctx'), None, 'tp'), may hold values from -0.15625 to 0.15625
- w_forget: bfloat16 [1536, 24], P(('shard', 'ctx'), 'tp'), may hold values from -0.15625 to 0.15625
- forget_bias: float32 [24], replicated, may hold values from 3 to 8
- w_ogate: bfloat16 [1536, 1536], P(('shard', 'ctx'), 'tp'), may hold values from -0.15625 to 0.15625
- w_out: bfloat16 [1536, 1536], P(('shard', 'ctx'), 'tp'), may hold values from -0.625 to 0.625
- w_gu: bfloat16 [1536, 2, 4096], P(('shard', 'ctx'), None, 'tp'), may hold values from -0.15625 to 0.15625
- w_down: bfloat16 [1536, 4096], P(('shard', 'ctx'), 'tp'), may hold values from -0.09375 to 0.09375
- gain_attn: float32 [1536], replicated, may hold values from 0.5 to 1.5
- gain_mlp: float32 [1536], replicated, may hold values from 0.5 to 1.5
- qk_gain: float32 [2, 64], replicated, may hold values from 1 to 2
Outputs:
- output: bfloat16 [4, 1024, 1536], P('shard', ('ctx', 'tp'))
- input_grad: bfloat16 [4, 1024, 1536], P('shard', ('ctx', 'tp'))
- grad_qkv: float32 [1536, 3, 1536], P(('shard', 'ctx'), None, 'tp')
- grad_forget: float32 [1536, 24], P(('shard', 'ctx'), 'tp')
- grad_forget_bias: float32 [24], replicated
- grad_ogate: float32 [1536, 1536], P(('shard', 'ctx'), 'tp')
- grad_out: float32 [1536, 1536], P(('shard', 'ctx'), 'tp')
- grad_gu: float32 [1536, 2, 4096], P(('shard', 'ctx'), None, 'tp')
- grad_down: float32 [1536, 4096], P(('shard', 'ctx'), 'tp')
- grad_gain_attn: float32 [1536], replicated
- grad_gain_mlp: float32 [1536], replicated
- grad_qk_gain: float32 [2, 64], replicated
Inputs may be any that keep to these rules, and one draw needn't show every extreme that they name: `lengths`: real tokens of a slot; positions at or past it are padding; both the least and the most value occur in every draw.
All inputs are finite; a program needn't handle non-finite values.
Results may differ from a plain program's by a relative error of at most 0.04.
Values may be sent and summed in bfloat16 or wider, within the bound.
No kernel may reach another device: no remote copies, remote signals or barrier semaphores. Data moves between devices by JAX's collectives and lax.ppermute only.
A program may use at most 128 MiB of HBM per device.

v0:
```python
import math
import jax
import jax.numpy as jnp
from jax import lax
from jax.sharding import PartitionSpec as P

epsilon = 1e-06


def shifted(block, axis, distance):
    devices = range(lax.axis_size(axis))
    route = [(i - distance, i) for i in devices if i - distance in devices]
    return lax.ppermute(block, axis, route)


def norm_rows(values, gain):
    return values * lax.rsqrt(jnp.mean(values * values, axis=-1, keepdims=True) + epsilon) * gain


def product(left, right):
    return jnp.dot(left, right, preferred_element_type=jnp.float32)


def product_t(left, right):
    return lax.dot_general(
        left, right, (((1,), (1,)), ((), ())), preferred_element_type=jnp.float32
    )


def outer_rows(left, right):
    return lax.dot_general(
        left, right, (((0,), (0,)), ((), ())), preferred_element_type=jnp.float32
    )


def body(
    tokens,
    cotangent,
    lengths,
    w_qkv,
    w_forget,
    forget_bias,
    w_ogate,
    w_out,
    w_gu,
    w_down,
    gain_attn,
    gain_mlp,
    qk_gain,
):
    slot_count, own_rows, model_width = tokens.shape
    tensor_size = lax.axis_size("tp")
    tensor_place = lax.axis_index("tp")
    span_index = lax.axis_index("ctx")
    half_rows = own_rows * tensor_size
    row_count = slot_count * half_rows
    local_heads = w_forget.shape[1]
    head_size = qk_gain.shape[1]
    head_cols = local_heads * head_size
    hidden_units = w_down.shape[1]
    item_count = slot_count * local_heads
    score_scale = 1.0 / math.sqrt(head_size)
    own_start = tensor_place * own_rows
    full_tokens, full_cot = (
        lax.all_gather(tokens, "tp", axis=1, tiled=True),
        lax.all_gather(cotangent, "tp", axis=1, tiled=True),
    )
    qkv_full, forget_full, ogate_full, out_full, gu_full, down_full = (
        lax.all_gather(w_qkv, ("shard", "ctx"), axis=0, tiled=True),
        lax.all_gather(w_forget, ("shard", "ctx"), axis=0, tiled=True),
        lax.all_gather(w_ogate, ("shard", "ctx"), axis=0, tiled=True),
        lax.all_gather(w_out, ("shard", "ctx"), axis=0, tiled=True),
        lax.all_gather(w_gu, ("shard", "ctx"), axis=0, tiled=True),
        lax.all_gather(w_down, ("shard", "ctx"), axis=0, tiled=True),
    )
    qkv_flat = qkv_full.reshape(model_width, 3 * head_cols)
    gu_flat = gu_full.reshape(model_width, 2 * hidden_units)

    def own_slice(values):
        return lax.dynamic_slice_in_dim(
            values.reshape(slot_count, half_rows, values.shape[-1]), own_start, own_rows, 1
        )

    positions = span_index * half_rows + jnp.arange(half_rows, dtype=jnp.int32)
    valid_rows = (positions[None, :] < lengths[:, None]).astype(jnp.float32).reshape(row_count, 1)
    own_positions = span_index * half_rows + own_start + jnp.arange(own_rows, dtype=jnp.int32)
    valid_own = (own_positions[None, :] < lengths[:, None]).astype(jnp.float32)[:, :, None]
    residual = full_tokens.reshape(row_count, model_width).astype(jnp.float32)
    normed = norm_rows(residual, gain_attn).astype(jnp.bfloat16)
    qkv_rows = product(normed, qkv_flat).reshape(row_count, 3, head_cols)
    query_raw = qkv_rows[:, 0].reshape(row_count, local_heads, head_size)
    key_raw = qkv_rows[:, 1].reshape(row_count, local_heads, head_size)
    queries = (
        norm_rows(query_raw, qk_gain[0])
        .astype(jnp.bfloat16)
        .reshape(slot_count, half_rows, head_cols)
    )
    keys_here = (
        norm_rows(key_raw, qk_gain[1])
        .astype(jnp.bfloat16)
        .reshape(slot_count, half_rows, head_cols)
    )
    values_here = qkv_rows[:, 2].astype(jnp.bfloat16).reshape(slot_count, half_rows, head_cols)
    bias_here = lax.dynamic_slice_in_dim(forget_bias, tensor_place * local_heads, local_heads)
    forget_pre = (product(normed, forget_full) + bias_here).reshape(
        slot_count, half_rows, local_heads
    )
    cum_here = jnp.cumsum(jax.nn.log_sigmoid(forget_pre), axis=1)
    keys_left, values_left = shifted((keys_here, values_here), "ctx", 1)
    cum_left = shifted(cum_here, "ctx", 1)
    cum_query = cum_here + cum_left[:, -1:, :]

    def by_head(values):
        shaped = values.reshape(slot_count, half_rows, local_heads, head_size)
        return jnp.transpose(shaped, (0, 2, 1, 3)).reshape(item_count, half_rows, head_size)

    def by_head_cum(values):
        return jnp.transpose(values, (0, 2, 1)).reshape(item_count, half_rows)

    def to_slots(values):
        shaped = values.reshape(slot_count, local_heads, half_rows, head_size)
        return jnp.transpose(shaped, (0, 2, 1, 3)).reshape(slot_count, half_rows, head_cols)

    def to_slots_cum(values):
        return jnp.transpose(values.reshape(slot_count, local_heads, half_rows), (0, 2, 1))

    q_items = by_head(queries)
    k_items = jnp.concatenate([by_head(keys_left), by_head(keys_here)], axis=1)
    v_items = jnp.concatenate([by_head(values_left), by_head(values_here)], axis=1)
    cq_items = by_head_cum(cum_query)
    ck_items = jnp.concatenate([by_head_cum(cum_left), cq_items], axis=1)
    place_ids = jnp.arange(half_rows, dtype=jnp.int32)
    earlier = jnp.broadcast_to(span_index > 0, (half_rows, half_rows))
    allowed = jnp.concatenate([earlier, place_ids[None, :] <= place_ids[:, None]], axis=1)

    def score_block(query_block, key_block, cum_rows, cum_cols):
        score_raw = (
            product_t(query_block, key_block) * score_scale + cum_rows[:, None] - cum_cols[None, :]
        )
        return jnp.where(allowed, score_raw, -jnp.inf)

    def forward_item(pieces):
        query_block, key_block, value_block, cum_rows, cum_cols = pieces
        score_vals = score_block(query_block, key_block, cum_rows, cum_cols)
        row_max = jnp.max(score_vals, axis=1, keepdims=True)
        expo = jnp.exp(score_vals - row_max)
        row_total = jnp.sum(expo, axis=1, keepdims=True)
        attn_probs = (expo / row_total).astype(jnp.bfloat16)
        return (product(attn_probs, value_block), (row_max + jnp.log(row_total))[:, 0])

    attended_items, lse_items = lax.map(
        forward_item, (q_items, k_items, v_items, cq_items, ck_items)
    )
    attended_rows = to_slots(attended_items).reshape(row_count, head_cols)
    opener = jax.nn.sigmoid(product(normed, ogate_full))
    gated = (attended_rows * opener).astype(jnp.bfloat16)
    branch_part = product_t(gated, out_full)
    branch_full = lax.psum(branch_part, "tp")
    middle = residual + branch_full
    middle_share = own_slice(middle)
    normed_mid = norm_rows(middle, gain_mlp).astype(jnp.bfloat16)
    both = product(normed_mid, gu_flat).reshape(row_count, 2, hidden_units)
    gate_pre = both[:, 0]
    up_pre = both[:, 1]
    gate_sig = jax.nn.sigmoid(gate_pre)
    hidden = (gate_pre * gate_sig * up_pre).astype(jnp.bfloat16)
    down_share = lax.psum_scatter(
        product_t(hidden, down_full)
        .reshape(slot_count, half_rows, model_width)
        .astype(jnp.bfloat16),
        "tp",
        scatter_dimension=1,
        tiled=True,
    ).astype(jnp.float32)
    output = (valid_own * (middle_share + down_share)).astype(jnp.bfloat16)
    cot_rows = full_cot.reshape(row_count, model_width) * valid_rows.astype(jnp.bfloat16)
    d_hidden = product(cot_rows, down_full)
    d_gate = d_hidden * up_pre * gate_sig * (1.0 + gate_pre * (1.0 - gate_sig))
    d_up = d_hidden * gate_pre * gate_sig
    d_both = (
        jnp.stack([d_gate, d_up], axis=1).astype(jnp.bfloat16).reshape(row_count, 2 * hidden_units)
    )
    grad_down = outer_rows(cot_rows, hidden)
    grad_gu = outer_rows(normed_mid, d_both).reshape(model_width, 2, hidden_units)
    d_mid_terms = product_t(d_both, gu_flat)
    d_normed_mid = lax.psum(d_mid_terms, "tp")
    _, pull_mid = jax.vjp(norm_rows, middle, gain_mlp)
    d_middle_norm, d_gain_mlp_all = pull_mid(d_normed_mid)
    d_middle = d_middle_norm + cot_rows.astype(jnp.float32)
    feat_share = model_width // tensor_size
    owner = jnp.arange(model_width, dtype=jnp.int32) // feat_share == tensor_place
    d_gain_mlp_own = jnp.where(owner, d_gain_mlp_all, 0.0)
    d_branch = d_middle.astype(jnp.bfloat16)
    d_middle_share = own_slice(d_middle)
    d_gated = product(d_branch, out_full)
    grad_out = outer_rows(d_branch, gated)
    d_attended = (d_gated * opener).astype(jnp.bfloat16)
    d_open = (d_gated * attended_rows * opener * (1.0 - opener)).astype(jnp.bfloat16)
    grad_ogate = outer_rows(normed, d_open)
    da_items = by_head(d_attended.reshape(slot_count, half_rows, head_cols))

    def backward_item(pieces):
        query_block, key_block, value_block, cum_rows, cum_cols, lse_block, grad_block = pieces
        score_vals = score_block(query_block, key_block, cum_rows, cum_cols)
        attn_probs = jnp.exp(score_vals - lse_block[:, None])
        d_probs = product_t(grad_block, value_block)
        centre = jnp.sum(attn_probs * d_probs, axis=1, keepdims=True)
        d_scores = (attn_probs * (d_probs - centre)).astype(jnp.bfloat16)
        d_query_block = product(d_scores, key_block) * score_scale
        d_key_block = outer_rows(d_scores, query_block) * score_scale
        d_value_block = outer_rows(attn_probs.astype(jnp.bfloat16), grad_block)
        d_cum_rows = jnp.sum(d_scores, axis=1, dtype=jnp.float32)
        d_cum_cols = -jnp.sum(d_scores, axis=0, dtype=jnp.float32)
        return (d_query_block, d_key_block, d_value_block, d_cum_rows, d_cum_cols)

    dq_items, dk_items, dv_items, dcq_items, dck_items = lax.map(
        backward_item, (q_items, k_items, v_items, cq_items, ck_items, lse_items, da_items)
    )
    dc_own = dcq_items + dck_items[:, half_rows:]
    dc_left = dck_items[:, :half_rows]
    dc_left = dc_left.at[:, -1].add(jnp.sum(dc_own, axis=1))
    back_keys, back_values, back_cum = (
        shifted(to_slots(dk_items[:, :half_rows]).astype(jnp.bfloat16), "ctx", -1).astype(
            jnp.float32
        ),
        shifted(to_slots(dv_items[:, :half_rows]).astype(jnp.bfloat16), "ctx", -1).astype(
            jnp.float32
        ),
        shifted(to_slots_cum(dc_left).astype(jnp.bfloat16), "ctx", -1).astype(jnp.float32),
    )
    d_query = to_slots(dq_items).reshape(row_count, local_heads, head_size)
    d_key = (to_slots(dk_items[:, half_rows:]) + back_keys).reshape(
        row_count, local_heads, head_size
    )
    d_value = (to_slots(dv_items[:, half_rows:]) + back_values).reshape(row_count, head_cols)
    d_cum = to_slots_cum(dc_own) + back_cum
    d_log = jnp.flip(jnp.cumsum(jnp.flip(d_cum, 1), axis=1), 1)
    d_forget = d_log * jax.nn.sigmoid(-forget_pre)
    d_bias_own = jnp.sum(d_forget, axis=(0, 1))
    d_forget_low = d_forget.reshape(row_count, local_heads).astype(jnp.bfloat16)
    grad_forget = outer_rows(normed, d_forget_low)
    _, pull_query = jax.vjp(norm_rows, query_raw, qk_gain[0])
    d_query_raw, d_query_gain = pull_query(d_query)
    _, pull_key = jax.vjp(norm_rows, key_raw, qk_gain[1])
    d_key_raw, d_key_gain = pull_key(d_key)
    d_mixed = (
        jnp.stack(
            [
                d_query_raw.reshape(row_count, head_cols),
                d_key_raw.reshape(row_count, head_cols),
                d_value,
            ],
            axis=1,
        )
        .astype(jnp.bfloat16)
        .reshape(row_count, 3 * head_cols)
    )
    grad_qkv = outer_rows(normed, d_mixed).reshape(model_width, 3, head_cols)
    d_normed = (
        product_t(d_mixed, qkv_flat)
        + product_t(d_open, ogate_full)
        + product_t(d_forget_low, forget_full)
    )
    root = lax.rsqrt(jnp.mean(residual * residual, axis=1, keepdims=True) + epsilon)
    unit = residual * root
    d_unit = d_normed * gain_attn
    dot_part = (jnp.sum(d_unit * unit, axis=1) / model_width).reshape(slot_count, half_rows)
    d_unit_share, dot_full = (
        lax.psum_scatter(
            d_unit.reshape(slot_count, half_rows, model_width).astype(jnp.bfloat16),
            "tp",
            scatter_dimension=1,
            tiled=True,
        ).astype(jnp.float32),
        lax.psum_scatter(
            dot_part.astype(jnp.bfloat16), "tp", scatter_dimension=1, tiled=True
        ).astype(jnp.float32),
    )
    unit_share = own_slice(unit)
    root_share = own_slice(root)
    input_grad = (
        d_middle_share + root_share * (d_unit_share - unit_share * dot_full[:, :, None])
    ).astype(jnp.bfloat16)
    grad_parts = (
        lax.psum_scatter(
            grad_qkv.astype(jnp.bfloat16), ("shard", "ctx"), scatter_dimension=0, tiled=True
        ).astype(jnp.float32),
        lax.psum_scatter(
            grad_forget.astype(jnp.bfloat16), ("shard", "ctx"), scatter_dimension=0, tiled=True
        ).astype(jnp.float32),
        lax.psum_scatter(
            grad_ogate.astype(jnp.bfloat16), ("shard", "ctx"), scatter_dimension=0, tiled=True
        ).astype(jnp.float32),
        lax.psum_scatter(
            grad_out.astype(jnp.bfloat16), ("shard", "ctx"), scatter_dimension=0, tiled=True
        ).astype(jnp.float32),
        lax.psum_scatter(
            grad_gu.astype(jnp.bfloat16), ("shard", "ctx"), scatter_dimension=0, tiled=True
        ).astype(jnp.float32),
        lax.psum_scatter(
            grad_down.astype(jnp.bfloat16), ("shard", "ctx"), scatter_dimension=0, tiled=True
        ).astype(jnp.float32),
    )
    bias_full = lax.dynamic_update_slice_in_dim(
        jnp.zeros(forget_bias.shape, jnp.float32), d_bias_own, tensor_place * local_heads, 0
    )
    gain_attn_part = jnp.sum(d_normed * unit, axis=0)
    small_parts = lax.psum(
        (gain_attn_part, d_gain_mlp_own, jnp.stack([d_query_gain, d_key_gain]), bias_full),
        ("shard", "ctx", "tp"),
    )
    return (
        output,
        input_grad,
        grad_parts[0],
        grad_parts[1],
        small_parts[3],
        grad_parts[2],
        grad_parts[3],
        grad_parts[4],
        grad_parts[5],
        small_parts[0],
        small_parts[1],
        small_parts[2],
    )


def solution(mesh):
    return jax.shard_map(
        body,
        mesh=mesh,
        in_specs=(
            P("shard", ("ctx", "tp"), None),
            P("shard", ("ctx", "tp"), None),
            P("shard"),
            P(("shard", "ctx"), None, "tp"),
            P(("shard", "ctx"), "tp"),
            P(),
            P(("shard", "ctx"), "tp"),
            P(("shard", "ctx"), "tp"),
            P(("shard", "ctx"), None, "tp"),
            P(("shard", "ctx"), "tp"),
            P(),
            P(),
            P(),
        ),
        out_specs=(
            P("shard", ("ctx", "tp"), None),
            P("shard", ("ctx", "tp"), None),
            P(("shard", "ctx"), None, "tp"),
            P(("shard", "ctx"), "tp"),
            P(),
            P(("shard", "ctx"), "tp"),
            P(("shard", "ctx"), "tp"),
            P(("shard", "ctx"), None, "tp"),
            P(("shard", "ctx"), "tp"),
            P(),
            P(),
            P(),
        ),
        check_vma=False,
    )
```

profile of v0, /device:TPU:0, one launch (start us, length us, event | category | flops | bytes accessed | tf_op | source)
XLA Modules:
  0.0 1049.7 jit_solution(11627350117377922482)
XLA Ops:
  11.9 10.6 %all-gather = bf16[8,192,6]{1,2,0:T(8,128)(2,1)S(1)} all-gather(bf16[1,192,6]{1,2,0:T(8,128)(2,1)} %bitcast.510), channel_id=1, replica_groups=mesh['shard'=4,'ctx'=2,'tp'=4] {'shard','ctx'}, dimensions={0}, use_global_device_ids=true | all-gather | bytes 20736 | tf_op jit(solution)/shard_map/all_gather | solution.py:70
  24.6 24.8 %all-gather.9.cloned.1.call-done = bf16[1,512,1536]{2,1,0:T(8,128)(2,1)} async-done(((bf16[1,128,1536]{2,1,0:T(8,128)(2,1)}), bf16[1,512,1536]{2,1,0:T(8,128)(2,1)}) %all-gather.9.cloned.1.call-update) | async-done | bytes 1572880 | tf_op jit(solution)/shard_map/all_gather | solution.py:65
  59.5 24.7 %all-gather.11.cloned.1.call-done = bf16[1536,3,384]{2,0,1:T(8,128)(2,1)} async-done(((bf16[192,3,384]{2,0,1:T(8,128)(2,1)}), bf16[1536,3,384]{2,0,1:T(8,128)(2,1)}) %all-gather.11.cloned.1.call-update) | async-done | bytes 3538960 | tf_op jit(solution)/shard_map/all_gather | solution.py:69
  84.2 6.1 copy.92
  90.3 4.1 fusion.41
  118.7 37.0 %while.31 = (s32[]{:T(128)}, f32[6,512,64]{1,2,0:T(8,128)}, f32[6,512]{1,0:T(8,128)S(1)}, bf16[6,512,64]{2,1,0:T(8,128)(2,1)}, bf16[6,1024,64]{2,1,0:T(8,128)(2,...) while((s32[]{:T(128)}, f32[6,512,64]{1,2,0:T(8,128)}, ...), condition=%wide.region_8.9_spmd, body=%wide.region_5.8_spmd.sunk | while | flops 139460096 | bytes 7643265 | solution.py:151
  159.7 4.0 fusion.126
  168.9 116.0 %all-reduce.5.cloned.1.call-done = f32[512,1536]{1,0:T(8,128)} async-done(((f32[512,1536]{1,0:T(8,128)}), f32[512,1536]{1,0:T(8,128)}) %all-reduce.5.cloned.1.call-update) | async-done | bytes 3145744 | tf_op jit(solution)/shard_map/psum | solution.py:158
  289.3 42.5 %all-gather.17.cloned.1.call-done = bf16[1536,2,1024]{2,0,1:T(8,128)(2,1)} async-done(((bf16[192,2,1024]{2,0,1:T(8,128)(2,1)}), bf16[1536,2,1024]{2,0,1:T(8,128)(2,1)}) %all-gather.17.cloned.1.call-update) | async-done | bytes 6291472 | tf_op jit(solution)/shard_map/all_gather | solution.py:73
  331.8 8.7 copy.104
  340.5 8.1 fusion.36
  348.6 21.9 %all-gather.21.cloned.1.call-done = bf16[1,512,1536]{2,1,0:T(8,128)(2,1)} async-done(((bf16[1,128,1536]{2,1,0:T(8,128)(2,1)}), bf16[1,512,1536]{2,1,0:T(8,128)(2,1)}) %all-gather.21.cloned.1.call-update) | async-done | bytes 1572880 | tf_op jit(solution)/shard_map/all_gather | solution.py:66
  370.5 33.1 %all-gather.19.cloned.1.call-done = bf16[1536,1024]{1,0:T(8,128)(2,1)} async-done(((bf16[192,1024]{1,0:T(8,128)(2,1)}), bf16[1536,1024]{1,0:T(8,128)(2,1)}) %all-gather.19.cloned.1.call-update) | async-done | bytes 3145744 | tf_op jit(solution)/shard_map/all_gather | solution.py:74
  403.6 5.9 fusion.52
  410.9 8.0 convolution_bitcast_fusion.2
  423.5 6.7 fusion.47
  430.5 109.7 %all-reduce.7.cloned.1.call-done = f32[512,1536]{1,0:T(8,128)} async-done(((f32[512,1536]{1,0:T(8,128)}), f32[512,1536]{1,0:T(8,128)}) %all-reduce.7.cloned.1.call-update) | async-done | bytes 3145744 | tf_op jit(solution)/shard_map/psum | solution.py:186
  552.2 97.2 %while.32 = (s32[]{:T(128)}, f32[6,512,64]{1,2,0:T(8,128)}, f32[6,1024,64]{1,2,0:T(8,128)}, f32[6,1024,64]{1,2,0:T(8,128)}, f32[6,512]{1,0:T(8,128)}, /*index=5*...) while((s32[]{:T(128)}, f32[6,512,64]{1,2,0:T(8,128)}, ...), condition=%wide.region_18.19_spmd, body=%wide.region_14.18_spmd.sunk | while | flops 342981632 | bytes 20376776 | solution.py:216
  676.4 4.1 reduce-window.16
  711.4 3.4 multiply_reduce_fusion.2
  715.7 6.4 convolution_convert_fusion.2
  722.2 3.7 convolution_convert_fusion.5
  729.0 5.8 convolution_convert_fusion.1
  738.0 4.0 copy.114
  742.0 8.9 convolution_convert_fusion
  755.5 41.1 %all-reduce.1 = (f32[24]{0:T(128)}, f32[1536]{0:T(1024)}, f32[1536]{0:T(1024)}, f32[2,64]{1,0:T(2,128)}) all-reduce(f32[24]{0:T(128)S(1)} %dynamic_update_slice.28, f32[1536]{0:T(1024)S(1)} %get-tuple-element.207, f32[1536]{0:T(1024)S(1)} %fusion.108, ...), channel_id=1, replica_groups=mesh['shard'=4,'ctx'=2,'tp'=4] {'shard','ctx','tp'}, use_global_device_ids=true, to_apply=%region_30.31 | all-reduce | flops 3224 | bytes 25792 | tf_op jit(solution)/shard_map/psum | solution.py:308
  797.5 8.2 reduce-scatter.26.cloned.1.call-done
  807.7 37.9 %reduce-scatter.20.cloned.1.call-done = bf16[192,384]{1,0:T(8,128)(2,1)} async-done(((bf16[1536,384]{1,0:T(8,128)(2,1)}), bf16[192,384]{1,0:T(8,128)(2,1)}) %reduce-scatter.20.cloned.1.call-update) | async-done | bytes 147472 | tf_op jit(solution)/shard_map/reduce_scatter | solution.py:291
  847.2 38.6 %reduce-scatter.22.cloned.1.call-done = bf16[192,384]{1,0:T(8,128)(2,1)} async-done(((bf16[1536,384]{1,0:T(8,128)(2,1)}), bf16[192,384]{1,0:T(8,128)(2,1)}) %reduce-scatter.22.cloned.1.call-update) | async-done | bytes 147472 | tf_op jit(solution)/shard_map/reduce_scatter | solution.py:294
  887.5 36.4 %reduce-scatter.16.cloned.1.call-done = bf16[1,128,1536]{2,1,0:T(8,128)(2,1)} async-done(((bf16[1,512,1536]{2,1,0:T(8,128)(2,1)}), bf16[1,128,1536]{2,1,0:T(8,128)(2,1)}) %reduce-scatter.16.cloned.1.call-update) | async-done | bytes 393232 | tf_op jit(solution)/shard_map/reduce_scatter | solution.py:269
  926.1 48.2 %reduce-scatter.18.cloned.1.call-done = bf16[192,3,384]{2,0,1:T(8,128)(2,1)} async-done(((bf16[1536,3,384]{2,0,1:T(8,128)(2,1)}), bf16[192,3,384]{2,0,1:T(8,128)(2,1)}) %reduce-scatter.18.cloned.1.call-update) | async-done | bytes 442384 | tf_op jit(solution)/shard_map/reduce_scatter | solution.py:285
  976.3 63.0 %reduce-scatter.24.cloned.1.call-done = bf16[192,2,1024]{2,0,1:T(8,128)(2,1)} async-done(((bf16[1536,2,1024]{2,0,1:T(8,128)(2,1)}), bf16[192,2,1024]{2,0,1:T(8,128)(2,1)}) %reduce-scatter.24.cloned.1.call-update) | async-done | bytes 786448 | tf_op jit(solution)/shard_map/reduce_scatter | solution.py:297
  (435 shorter events, 288.3 us)
Async XLA Ops:
  7.2 17.4 %copy-start.69 = (f32[24]{0:T(128)S(1)}, f32[24]{0:T(128)}, u32[]{:S(2)}) copy-start(f32[24]{0:T(128)} %param.24) | copy-start | bytes 292
  7.2 42.2 %all-gather.9.cloned.1.call-start = ((), (), s32[]{:S(2)}) async-start(), calls=%async_computation.9 | async-start | bytes 1966080 | tf_op jit(solution)/shard_map/all_gather | solution.py:65
  7.9 76.3 %all-gather.11.cloned.1.call-start = ((), (), s32[]{:S(2)}) async-start(), calls=%async_computation.10 | async-start | bytes 3981312 | tf_op jit(solution)/shard_map/all_gather | solution.py:69
  8.7 42.5 %copy-start.59 = (f32[1536]{0:T(1024)S(1)}, f32[1536]{0:T(1024)}, u32[]{:S(2)}) copy-start(f32[1536]{0:T(1024)} %param.29) | copy-start | bytes 18436
  8.7 147.0 %all-gather.13.cloned.1.call-start = ((), (), s32[]{:S(2)}) async-start(), calls=%async_computation.11 | async-start | bytes 1327104 | tf_op jit(solution)/shard_map/all_gather | solution.py:71
  9.4 150.3 %all-gather.15.cloned.1.call-start = ((), (), s32[]{:S(2)}) async-start(), calls=%async_computation.12 | async-start | bytes 1327104 | tf_op jit(solution)/shard_map/all_gather | solution.py:72
  10.0 274.9 %all-reduce.5.cloned.1.call-start = ((), (), s32[]{:S(2)}) async-start(), calls=%async_computation.13 | async-start | bytes 6291456 | tf_op jit(solution)/shard_map/psum | solution.py:158
  11.5 84.3 %copy-start.49 = (f32[384]{0:T(512)}, f32[384]{0:T(512)S(1)}, u32[]{:S(2)}) copy-start(f32[384]{0:T(512)S(1)} %mul.513) | copy-start | bytes 4612
  22.7 30.5 %copy-start.39 = (bf16[1536,6]{0,1:T(8,128)(2,1)}, bf16[1536,6]{0,1:T(8,128)(2,1)S(1)}, u32[]{:S(2)}) copy-start(bf16[1536,6]{0,1:T(8,128)(2,1)S(1)} %reshape.771) | copy-start | bytes 55300
  51.2 39.1 %copy-start.57 = (f32[512]{0:T(512)}, f32[512]{0:T(512)S(1)}, u32[]{:S(2)}) copy-start(f32[512]{0:T(512)S(1)} %add_rsqrt_fusion) | copy-start | bytes 6148
  55.5 2.4 collective-permute-start.1
  59.5 30.8 %copy-start.2 = (bf16[1,512,1536]{2,1,0:T(8,128)(2,1)S(1)}, bf16[1,512,1536]{2,1,0:T(8,128)(2,1)}, u32[]{:S(2)}) copy-start(bf16[1,512,1536]{2,1,0:T(8,128)(2,1)} %all-gather.9.cloned.1.call-done) | copy-start | bytes 4718596
  94.6 9.4 copy-start.6
  96.7 13.4 %collective-permute-start = (bf16[1,512,384]{1,2,0:T(8,128)(2,1)}, bf16[1,512,384]{1,2,0:T(8,128)(2,1)}, u32[]{:S(2)}, u32[]{:S(2)}) collective-permute-start(bf16[1,512,384]{1,2,0:T(8,128)(2,1)} %multiply_convert_fusion.9), channel_id=1, source_target_pairs={{0,4},{1,5},{2,6},{3,7},{8,12},{9,13},{10,14},{11,15},{16,20},{17,... | collective-permute-start | bytes 1179656 | tf_op jit(solution)/shard_map/ppermute | solution.py:13
  99.6 12.7 %collective-permute-start.2 = (bf16[1,512,384]{1,2,0:T(8,128)(2,1)}, bf16[1,512,384]{1,2,0:T(8,128)(2,1)}, u32[]{:S(2)}, u32[]{:S(2)}) collective-permute-start(bf16[1,512,384]{1,2,0:T(8,128)(2,1)} %slice_bitcast_fusion.5), channel_id=1, source_target_pairs={{0,4},{1,5},{2,6},{3,7},{8,12},{9,13},{10,14},{11,15},{16,20},{17,... | collective-permute-start | bytes 1179656 | tf_op jit(solution)/shard_map/ppermute | solution.py:13
  163.7 168.1 %all-gather.17.cloned.1.call-start = ((), (), s32[]{:S(2)}) async-start(), calls=%async_computation.14 | async-start | bytes 7077888 | tf_op jit(solution)/shard_map/all_gather | solution.py:73
  165.9 204.6 %all-gather.21.cloned.1.call-start = ((), (), s32[]{:S(2)}) async-start(), calls=%async_computation.17 | async-start | bytes 1966080 | tf_op jit(solution)/shard_map/all_gather | solution.py:66
  166.7 236.9 %all-gather.19.cloned.1.call-start = ((), (), s32[]{:S(2)}) async-start(), calls=%async_computation.15 | async-start | bytes 3538944 | tf_op jit(solution)/shard_map/all_gather | solution.py:74
  167.4 372.7 %all-reduce.7.cloned.1.call-start = ((), (), s32[]{:S(2)}) async-start(), calls=%async_computation.18 | async-start | bytes 6291456 | tf_op jit(solution)/shard_map/psum | solution.py:186
  287.8 252.4 %copy-start = (f32[512,1536]{1,0:T(8,128)}, f32[512,1536]{1,0:T(8,128)S(1)}, u32[]{:S(2)}) copy-start(f32[512,1536]{1,0:T(8,128)S(1)} %get-tuple-element.267) | copy-start | bytes 9437188
  418.9 332.6 %reduce-scatter.14.cloned.1.call-start = ((), (), s32[]{:S(2)}) async-start(), calls=%async_computation.16 | async-start | bytes 1966080 | tf_op jit(solution)/shard_map/reduce_scatter | solution.py:167
  430.2 323.7 %reduce-scatter.30.cloned.1.call-start = ((), (), s32[]{:S(2)}) async-start(), calls=%async_computation.26 | async-start | bytes 442368
  653.4 51.8 %collective-permute-start.4 = (bf16[1,512,384]{1,2,0:T(8,128)(2,1)}, bf16[1,512,384]{1,2,0:T(8,128)(2,1)}, u32[]{:S(2)}, u32[]{:S(2)}) collective-permute-start(bf16[1,512,384]{1,2,0:T(8,128)(2,1)} %bitcast.100), channel_id=1, source_target_pairs={{4,0},{5,1},{6,2},{7,3},{12,8},{13,9},{14,10},{15,11},{20,16},{21,... | collective-permute-start | bytes 1179656 | tf_op jit(solution)/shard_map/ppermute | solution.py:13
  656.6 44.0 %collective-permute-start.3 = (bf16[1,512,384]{1,2,0:T(8,128)(2,1)}, bf16[1,512,384]{1,2,0:T(8,128)(2,1)}, u32[]{:S(2)}, u32[]{:S(2)}) collective-permute-start(bf16[1,512,384]{1,2,0:T(8,128)(2,1)} %bitcast.90), channel_id=1, source_target_pairs={{4,0},{5,1},{6,2},{7,3},{12,8},{13,9},{14,10},{15,11},{20,16},{21,... | collective-permute-start | bytes 1179656 | tf_op jit(solution)/shard_map/ppermute | solution.py:13
  665.8 6.0 collective-permute-start.5
  700.3 96.4 %reduce-scatter.28.cloned.1.call-start = ((), (), s32[]{:S(2)}) async-start(), calls=%async_computation.25 | async-start | bytes 163840
  715.7 90.0 %reduce-scatter.26.cloned.1.call-start = ((), (), s32[]{:S(2)}) async-start(), calls=%async_computation.24 | async-start | bytes 3538944 | tf_op jit(solution)/shard_map/reduce_scatter | solution.py:300
  722.2 123.4 %reduce-scatter.20.cloned.1.call-start = ((), (), s32[]{:S(2)}) async-start(), calls=%async_computation.21 | async-start | bytes 1327104 | tf_op jit(solution)/shard_map/reduce_scatter | solution.py:291
  725.9 159.9 %reduce-scatter.22.cloned.1.call-start = ((), (), s32[]{:S(2)}) async-start(), calls=%async_computation.22 | async-start | bytes 1327104 | tf_op jit(solution)/shard_map/reduce_scatter | solution.py:294
  728.0 195.8 %reduce-scatter.16.cloned.1.call-start = ((), (), s32[]{:S(2)}) async-start(), calls=%async_computation.19 | async-start | bytes 1966080 | tf_op jit(solution)/shard_map/reduce_scatter | solution.py:269
  728.6 245.7 %reduce-scatter.18.cloned.1.call-start = ((), (), s32[]{:S(2)}) async-start(), calls=%async_computation.20 | async-start | bytes 3981312 | tf_op jit(solution)/shard_map/reduce_scatter | solution.py:285
  734.9 304.4 %reduce-scatter.24.cloned.1.call-start = ((), (), s32[]{:S(2)}) async-start(), calls=%async_computation.23 | async-start | bytes 7077888 | tf_op jit(solution)/shard_map/reduce_scatter | solution.py:297
  (67 other events, 194.6 us)
Sparse Core Ops, SparseCore 0:
  9.6 39.7 all-gather.8
  51.3 32.8 all-gather.10
  86.1 24.0 all-gather.12
  112.0 24.0 all-gather.14
  163.8 121.0 all-reduce.4
  287.2 44.5 all-gather.16
  333.4 37.0 all-gather.20
  372.4 31.1 all-gather.18
  419.0 121.0 all-reduce.6
  542.3 34.2 reduce-scatter.13
  700.4 35.1 reduce-scatter.29
  738.2 19.1 reduce-scatter.27
  761.2 44.4 reduce-scatter.25
  808.8 36.7 reduce-scatter.19
  849.0 36.7 reduce-scatter.21
  888.6 35.2 reduce-scatter.15
  927.2 47.0 reduce-scatter.17
  977.5 61.7 reduce-scatter.23
where the time goes:
time: 1060 us; the launch traced here: 1050 us
  waiting for transfers between devices  611 us (58%)
  matrix products  162 us (15%)
  local copies, waits for them, and re-layouts  121 us (11%)
  other arithmetic  75.4 us (7%)
  blocking collectives  51.8 us (5%)
  between operations  16.4 us (2%)
  starting transfers between devices  12.2 us (1%)
    psum x1, waiting for transfers between devices, body(): branch_full = lax.psum(branch_part, 'tp')  116 us
    psum x1, waiting for transfers between devices, body(): d_normed_mid = lax.psum(d_mid_terms, 'tp')  110 us
    reduce_scatter x1, waiting for transfers between devices, body(): lax.psum_scatter(grad_gu.astype(jnp.bfloat16), ('shard', 'ctx'), scatter_...  63 us
    dot_general x24, matrix products, product_t(): lax.dot_general(left, right, (((1,), (1,)), ((), ())), preferred_element_...  58 us
    dot_general x18, matrix products, outer_rows(): lax.dot_general(left, right, (((0,), (0,)), ((), ())), preferred_element_...  52.8 us
    dot_general x18, matrix products, product(): return jnp.dot(left, right, preferred_element_type=jnp.float32)  51.2 us
    reduce_scatter x1, waiting for transfers between devices, body(): lax.psum_scatter(grad_qkv.astype(jnp.bfloat16), ('shard', 'ctx'), scatter...  48.2 us
    all_gather x1, waiting for transfers between devices, body(): lax.all_gather(w_gu, ('shard', 'ctx'), axis=0, tiled=True)  42.5 us
  transfers between devices with their start and end apart: 24, of which 14 were waited for; matrix products, arithmetic and copies ran while one was open for 31% of the time, Pallas kernels for 0%

commit v1 on v0

--- a/solution.py
+++ b/solution.py
@@ -5,6 +5,18 @@
 from jax.sharding import PartitionSpec as P
 
 epsilon = 1e-06
+
+
+def gather_by_bits(value, axis, dim):
+    ways, here = (lax.axis_size(axis), lax.axis_index(axis))
+    grown, reach = (value, 1)
+    while reach < ways:
+        theirs = lax.ppermute(grown, axis, [(d, d ^ reach) for d in range(ways)])
+        mine_first = jnp.concatenate([grown, theirs], axis=dim)
+        theirs_first = jnp.concatenate([theirs, grown], axis=dim)
+        grown = jnp.where(here & reach == 0, mine_first, theirs_first)
+        reach = 2 * reach
+    return grown
 
 
 def shifted(block, axis, distance):
@@ -71,7 +83,7 @@
         lax.all_gather(w_ogate, ("shard", "ctx"), axis=0, tiled=True),
         lax.all_gather(w_out, ("shard", "ctx"), axis=0, tiled=True),
         lax.all_gather(w_gu, ("shard", "ctx"), axis=0, tiled=True),
-        lax.all_gather(w_down, ("shard", "ctx"), axis=0, tiled=True),
+        gather_by_bits(w_down, ("shard", "ctx"), 0),
     )
     qkv_flat = qkv_full.reshape(model_width, 3 * head_cols)
     gu_flat = gu_full.reshape(model_width, 2 * hidden_units)

time: 1060 us -> 1030 us (0.972)
  waiting for transfers between devices: 611 us -> 571 us
    all_gather x1 -> x0, waiting for transfers between devices: 33.1 us -> none  [body(): lax.all_gather(w_down, ('shard', 'ctx'), axis=0, tiled=True)]
    psum x1, waiting for transfers between devices: 116 us -> 93.3 us  [body(): branch_full = lax.psum(branch_part, 'tp')]
    ppermute x0 -> x3, waiting for transfers between devices: none -> 19.2 us  [gather_by_bits(): theirs = lax.ppermute(grown, axis, [(d, d ^ reach) for d in range(ways)])]
  transfers between devices with their start and end apart: 24 -> 26, of which waited for: 14 -> 15; matrix products, arithmetic and copies ran while one was open for 31% -> 33% of each run, Pallas kernels for 0% -> 0%
where the time goes in v1:
time: 1030 us; the launch traced here: 1020 us
  waiting for transfers between devices  571 us (55%)
  matrix products  164 us (16%)
  local copies, waits for them, and re-layouts  121 us (12%)
  other arithmetic  77.5 us (8%)
  blocking collectives  51.8 us (5%)
  between operations  15.8 us (2%)
  starting transfers between devices  15 us (1%)
    psum x1, waiting for transfers between devices, body(): d_normed_mid = lax.psum(d_mid_terms, 'tp')  108 us
    psum x1, waiting for transfers between devices, body(): branch_full = lax.psum(branch_part, 'tp')  93.3 us
    reduce_scatter x1, waiting for transfers between devices, body(): lax.psum_scatter(grad_gu.astype(jnp.bfloat16), ('shard', 'ctx'), scatter_...  63 us
    dot_general x24, matrix products, product_t(): lax.dot_general(left, right, (((1,), (1,)), ((), ())), preferred_element_...  58.6 us
    dot_general x18, matrix products, outer_rows(): lax.dot_general(left, right, (((0,), (0,)), ((), ())), preferred_element_...  52.9 us
    dot_general x18, matrix products, product(): return jnp.dot(left, right, preferred_element_type=jnp.float32)  52.5 us
    reduce_scatter x1, waiting for transfers between devices, body(): lax.psum_scatter(grad_qkv.astype(jnp.bfloat16), ('shard', 'ctx'), scatter...  48.2 us
    all_gather x1, waiting for transfers between devices, body(): lax.all_gather(w_gu, ('shard', 'ctx'), axis=0, tiled=True)  42.5 us
  transfers between devices with their start and end apart: 26, of which 15 were waited for; matrix products, arithmetic and copies ran while one was open for 33% of the time, Pallas kernels for 0%

profile of v1, /device:TPU:0, one launch (start us, length us, event | category | flops | bytes accessed | tf_op | source)
XLA Modules:
  0.0 1016.2 jit_solution(10547970498878797645)
XLA Ops:
  12.1 10.6 %all-gather = bf16[8,192,6]{1,2,0:T(8,128)(2,1)S(1)} all-gather(bf16[1,192,6]{1,2,0:T(8,128)(2,1)} %bitcast.508), channel_id=1, replica_groups=mesh['shard'=4,'ctx'=2,'tp'=4] {'shard','ctx'}, dimensions={0}, use_global_device_ids=true | all-gather | bytes 20736 | tf_op jit(solution)/shard_map/all_gather | solution.py:82
  24.8 24.6 %all-gather.8.cloned.1.call-done = bf16[1,512,1536]{2,1,0:T(8,128)(2,1)} async-done(((bf16[1,128,1536]{2,1,0:T(8,128)(2,1)}), bf16[1,512,1536]{2,1,0:T(8,128)(2,1)}) %all-gather.8.cloned.1.call-update) | async-done | bytes 1572880 | tf_op jit(solution)/shard_map/all_gather | solution.py:77
  59.5 24.7 %all-gather.10.cloned.1.call-done = bf16[1536,3,384]{2,0,1:T(8,128)(2,1)} async-done(((bf16[192,3,384]{2,0,1:T(8,128)(2,1)}), bf16[1536,3,384]{2,0,1:T(8,128)(2,1)}) %all-gather.10.cloned.1.call-update) | async-done | bytes 3538960 | tf_op jit(solution)/shard_map/all_gather | solution.py:81
  84.2 6.0 copy.92
  90.3 4.1 fusion.41
  118.6 37.0 %while.31 = (s32[]{:T(128)}, f32[6,512,64]{1,2,0:T(8,128)}, f32[6,512]{1,0:T(8,128)S(1)}, bf16[6,512,64]{2,1,0:T(8,128)(2,1)}, bf16[6,1024,64]{2,1,0:T(8,128)(2,...) while((s32[]{:T(128)}, f32[6,512,64]{1,2,0:T(8,128)}, ...), condition=%wide.region_8.9_spmd, body=%wide.region_5.8_spmd.sunk | while | flops 139460096 | bytes 7643265 | solution.py:163
  156.2 3.4 fusion.84
  159.6 4.0 fusion.128
  170.4 17.5 %collective-permute-done.4 = bf16[384,1024]{1,0:T(8,128)(2,1)S(1)} collective-permute-done((bf16[384,1024]{1,0:T(8,128)(2,1)S(1)}, bf16[384,1024]{1,0:T(8,128)(2,1)S(1)}, u32[]{:S(2)}, u32[]{:S(2)}) %collective-permute-start.4) | collective-permute-done | bytes 786464 | tf_op jit(solution)/shard_map/ppermute | solution.py:14
  191.5 93.3 %all-reduce.5.cloned.1.call-done = f32[512,1536]{1,0:T(8,128)} async-done(((f32[512,1536]{1,0:T(8,128)}), f32[512,1536]{1,0:T(8,128)}) %all-reduce.5.cloned.1.call-update) | async-done | bytes 3145744 | tf_op jit(solution)/shard_map/psum | solution.py:170
  289.2 42.5 %all-gather.16.cloned.1.call-done = bf16[1536,2,1024]{2,0,1:T(8,128)(2,1)} async-done(((bf16[192,2,1024]{2,0,1:T(8,128)(2,1)}), bf16[1536,2,1024]{2,0,1:T(8,128)(2,1)}) %all-gather.16.cloned.1.call-update) | async-done | bytes 6291472 | tf_op jit(solution)/shard_map/all_gather | solution.py:85
  331.7 8.7 copy.104
  340.4 8.1 fusion.36
  348.4 22.0 %all-gather.18.cloned.1.call-done = bf16[1,512,1536]{2,1,0:T(8,128)(2,1)} async-done(((bf16[1,128,1536]{2,1,0:T(8,128)(2,1)}), bf16[1,512,1536]{2,1,0:T(8,128)(2,1)}) %all-gather.18.cloned.1.call-update) | async-done | bytes 1572880 | tf_op jit(solution)/shard_map/all_gather | solution.py:78
  370.4 7.1 fusion.52
  378.8 8.0 convolution_bitcast_fusion.2
  391.6 7.3 fusion.47
  399.2 107.8 %all-reduce.7.cloned.1.call-done = f32[512,1536]{1,0:T(8,128)} async-done(((f32[512,1536]{1,0:T(8,128)}), f32[512,1536]{1,0:T(8,128)}) %all-reduce.7.cloned.1.call-update) | async-done | bytes 3145744 | tf_op jit(solution)/shard_map/psum | solution.py:198
  519.0 97.3 %while.32 = (s32[]{:T(128)}, f32[6,512,64]{1,2,0:T(8,128)}, f32[6,1024,64]{1,2,0:T(8,128)}, f32[6,1024,64]{1,2,0:T(8,128)}, f32[6,512]{1,0:T(8,128)}, /*index=5*...) while((s32[]{:T(128)}, f32[6,512,64]{1,2,0:T(8,128)}, ...), condition=%wide.region_18.19_spmd, body=%wide.region_14.18_spmd.sunk | while | flops 342981632 | bytes 20376776 | solution.py:228
  643.4 4.1 reduce-window.16
  682.7 6.4 convolution_convert_fusion.2
  689.2 3.7 convolution_convert_fusion.5
  696.1 5.8 convolution_convert_fusion.1
  705.1 4.0 copy.114
  709.0 8.9 convolution_convert_fusion
  722.6 41.1 %all-reduce.1 = (f32[24]{0:T(128)}, f32[1536]{0:T(1024)}, f32[1536]{0:T(1024)}, f32[2,64]{1,0:T(2,128)}) all-reduce(f32[24]{0:T(128)S(1)} %dynamic_update_slice.28, f32[1536]{0:T(1024)S(1)} %get-tuple-element.207, f32[1536]{0:T(1024)S(1)} %fusion.108, ...), channel_id=1, replica_groups=mesh['shard'=4,'ctx'=2,'tp'=4] {'shard','ctx','tp'}, use_global_device_ids=true, to_apply=%region_30.31 | all-reduce | flops 3224 | bytes 25792 | tf_op jit(solution)/shard_map/psum | solution.py:320
  764.6 8.1 reduce-scatter.26.cloned.1.call-done
  774.6 38.1 %reduce-scatter.20.cloned.1.call-done = bf16[192,384]{1,0:T(8,128)(2,1)} async-done(((bf16[1536,384]{1,0:T(8,128)(2,1)}), bf16[192,384]{1,0:T(8,128)(2,1)}) %reduce-scatter.20.cloned.1.call-update) | async-done | bytes 147472 | tf_op jit(solution)/shard_map/reduce_scatter | solution.py:303
  814.3 38.6 %reduce-scatter.22.cloned.1.call-done = bf16[192,384]{1,0:T(8,128)(2,1)} async-done(((bf16[1536,384]{1,0:T(8,128)(2,1)}), bf16[192,384]{1,0:T(8,128)(2,1)}) %reduce-scatter.22.cloned.1.call-update) | async-done | bytes 147472 | tf_op jit(solution)/shard_map/reduce_scatter | solution.py:306
  854.6 36.4 %reduce-scatter.16.cloned.1.call-done = bf16[1,128,1536]{2,1,0:T(8,128)(2,1)} async-done(((bf16[1,512,1536]{2,1,0:T(8,128)(2,1)}), bf16[1,128,1536]{2,1,0:T(8,128)(2,1)}) %reduce-scatter.16.cloned.1.call-update) | async-done | bytes 393232 | tf_op jit(solution)/shard_map/reduce_scatter | solution.py:281
  893.1 48.2 %reduce-scatter.18.cloned.1.call-done = bf16[192,3,384]{2,0,1:T(8,128)(2,1)} async-done(((bf16[1536,3,384]{2,0,1:T(8,128)(2,1)}), bf16[192,3,384]{2,0,1:T(8,128)(2,1)}) %reduce-scatter.18.cloned.1.call-update) | async-done | bytes 442384 | tf_op jit(solution)/shard_map/reduce_scatter | solution.py:297
  943.4 63.0 %reduce-scatter.24.cloned.1.call-done = bf16[192,2,1024]{2,0,1:T(8,128)(2,1)} async-done(((bf16[1536,2,1024]{2,0,1:T(8,128)(2,1)}), bf16[192,2,1024]{2,0,1:T(8,128)(2,1)}) %reduce-scatter.24.cloned.1.call-update) | async-done | bytes 786448 | tf_op jit(solution)/shard_map/reduce_scatter | solution.py:309
  (442 shorter events, 293.9 us)
Async XLA Ops:
  7.2 42.2 %all-gather.8.cloned.1.call-start = ((), (), s32[]{:S(2)}) async-start(), calls=%async_computation.9 | async-start | bytes 1966080 | tf_op jit(solution)/shard_map/all_gather | solution.py:77
  7.9 76.3 %all-gather.10.cloned.1.call-start = ((), (), s32[]{:S(2)}) async-start(), calls=%async_computation.10 | async-start | bytes 3981312 | tf_op jit(solution)/shard_map/all_gather | solution.py:81
  8.7 42.5 %copy-start.60 = (f32[1536]{0:T(1024)S(1)}, f32[1536]{0:T(1024)}, u32[]{:S(2)}) copy-start(f32[1536]{0:T(1024)} %param.29) | copy-start | bytes 18436
  8.7 146.9 %all-gather.12.cloned.1.call-start = ((), (), s32[]{:S(2)}) async-start(), calls=%async_computation.11 | async-start | bytes 1327104 | tf_op jit(solution)/shard_map/all_gather | solution.py:83
  9.4 150.2 %all-gather.14.cloned.1.call-start = ((), (), s32[]{:S(2)}) async-start(), calls=%async_computation.12 | async-start | bytes 1327104 | tf_op jit(solution)/shard_map/all_gather | solution.py:84
  10.0 274.8 %all-reduce.5.cloned.1.call-start = ((), (), s32[]{:S(2)}) async-start(), calls=%async_computation.13 | async-start | bytes 6291456 | tf_op jit(solution)/shard_map/psum | solution.py:170
  11.5 84.2 %copy-start.50 = (f32[384]{0:T(512)}, f32[384]{0:T(512)S(1)}, u32[]{:S(2)}) copy-start(f32[384]{0:T(512)S(1)} %mul.516) | copy-start | bytes 4612
  22.8 30.4 %copy-start.40 = (bf16[1536,6]{0,1:T(8,128)(2,1)}, bf16[1536,6]{0,1:T(8,128)(2,1)S(1)}, u32[]{:S(2)}) copy-start(bf16[1536,6]{0,1:T(8,128)(2,1)S(1)} %reshape.771) | copy-start | bytes 55300
  51.2 39.0 %copy-start.58 = (f32[512]{0:T(512)}, f32[512]{0:T(512)S(1)}, u32[]{:S(2)}) copy-start(f32[512]{0:T(512)S(1)} %add_rsqrt_fusion) | copy-start | bytes 6148
  55.5 2.4 collective-permute-start.1
  59.5 30.8 %copy-start.2 = (bf16[1,512,1536]{2,1,0:T(8,128)(2,1)S(1)}, bf16[1,512,1536]{2,1,0:T(8,128)(2,1)}, u32[]{:S(2)}) copy-start(bf16[1,512,1536]{2,1,0:T(8,128)(2,1)} %all-gather.8.cloned.1.call-done) | copy-start | bytes 4718596
  96.6 13.3 %collective-permute-start = (bf16[1,512,384]{1,2,0:T(8,128)(2,1)}, bf16[1,512,384]{1,2,0:T(8,128)(2,1)}, u32[]{:S(2)}, u32[]{:S(2)}) collective-permute-start(bf16[1,512,384]{1,2,0:T(8,128)(2,1)} %multiply_convert_fusion.9), channel_id=1, source_target_pairs={{0,4},{1,5},{2,6},{3,7},{8,12},{9,13},{10,14},{11,15},{16,20},{17,... | collective-permute-start | bytes 1179656 | tf_op jit(solution)/shard_map/ppermute | solution.py:25
  99.5 12.6 %collective-permute-start.2 = (bf16[1,512,384]{1,2,0:T(8,128)(2,1)}, bf16[1,512,384]{1,2,0:T(8,128)(2,1)}, u32[]{:S(2)}, u32[]{:S(2)}) collective-permute-start(bf16[1,512,384]{1,2,0:T(8,128)(2,1)} %slice_bitcast_fusion.5), channel_id=1, source_target_pairs={{0,4},{1,5},{2,6},{3,7},{8,12},{9,13},{10,14},{11,15},{16,20},{17,... | collective-permute-start | bytes 1179656 | tf_op jit(solution)/shard_map/ppermute | solution.py:25
  163.6 168.1 %all-gather.16.cloned.1.call-start = ((), (), s32[]{:S(2)}) async-start(), calls=%async_computation.14 | async-start | bytes 7077888 | tf_op jit(solution)/shard_map/all_gather | solution.py:85
  165.8 204.5 %all-gather.18.cloned.1.call-start = ((), (), s32[]{:S(2)}) async-start(), calls=%async_computation.16 | async-start | bytes 1966080 | tf_op jit(solution)/shard_map/all_gather | solution.py:78
  166.1 1.8 collective-permute-start.3
  168.2 19.6 %collective-permute-start.4 = (bf16[384,1024]{1,0:T(8,128)(2,1)S(1)}, bf16[384,1024]{1,0:T(8,128)(2,1)S(1)}, u32[]{:S(2)}, u32[]{:S(2)}) collective-permute-start(bf16[384,1024]{1,0:T(8,128)(2,1)S(1)} %maximum_select_fusion.2), channel_id=1, source_target_pairs={{0,8},{4,12},{8,0},{12,4},{16,24},{20,28},{24,16},{28,20},{1,9},{5... | collective-permute-start | bytes 2359304 | tf_op jit(solution)/shard_map/ppermute | solution.py:14
  169.7 337.3 %all-reduce.7.cloned.1.call-start = ((), (), s32[]{:S(2)}) async-start(), calls=%async_computation.17 | async-start | bytes 6291456 | tf_op jit(solution)/shard_map/psum | solution.py:198
  189.6 180.8 %collective-permute-start.5 = (bf16[768,1024]{1,0:T(8,128)(2,1)}, bf16[768,1024]{1,0:T(8,128)(2,1)}, u32[]{:S(2)}, u32[]{:S(2)}) collective-permute-start(bf16[768,1024]{1,0:T(8,128)(2,1)} %maximum_select_fusion.1), channel_id=1, source_target_pairs={{0,16},{4,20},{8,24},{12,28},{16,0},{20,4},{24,8},{28,12},{1,17},{... | collective-permute-start | bytes 4718600 | tf_op jit(solution)/shard_map/ppermute | solution.py:14
  287.7 219.3 %copy-start = (f32[512,1536]{1,0:T(8,128)}, f32[512,1536]{1,0:T(8,128)S(1)}, u32[]{:S(2)}) copy-start(f32[512,1536]{1,0:T(8,128)S(1)} %get-tuple-element.267) | copy-start | bytes 9437188
  386.9 331.7 %reduce-scatter.14.cloned.1.call-start = ((), (), s32[]{:S(2)}) async-start(), calls=%async_computation.15 | async-start | bytes 1966080 | tf_op jit(solution)/shard_map/reduce_scatter | solution.py:179
  398.9 322.0 %reduce-scatter.30.cloned.1.call-start = ((), (), s32[]{:S(2)}) async-start(), calls=%async_computation.25 | async-start | bytes 442368
  620.3 51.9 %collective-permute-start.7 = (bf16[1,512,384]{1,2,0:T(8,128)(2,1)}, bf16[1,512,384]{1,2,0:T(8,128)(2,1)}, u32[]{:S(2)}, u32[]{:S(2)}) collective-permute-start(bf16[1,512,384]{1,2,0:T(8,128)(2,1)} %bitcast.100), channel_id=1, source_target_pairs={{4,0},{5,1},{6,2},{7,3},{12,8},{13,9},{14,10},{15,11},{20,16},{21,... | collective-permute-start | bytes 1179656 | tf_op jit(solution)/shard_map/ppermute | solution.py:25
  623.6 44.0 %collective-permute-start.6 = (bf16[1,512,384]{1,2,0:T(8,128)(2,1)}, bf16[1,512,384]{1,2,0:T(8,128)(2,1)}, u32[]{:S(2)}, u32[]{:S(2)}) collective-permute-start(bf16[1,512,384]{1,2,0:T(8,128)(2,1)} %bitcast.90), channel_id=1, source_target_pairs={{4,0},{5,1},{6,2},{7,3},{12,8},{13,9},{14,10},{15,11},{20,16},{21,... | collective-permute-start | bytes 1179656 | tf_op jit(solution)/shard_map/ppermute | solution.py:25
  632.7 6.1 collective-permute-start.8
  667.1 96.6 %reduce-scatter.28.cloned.1.call-start = ((), (), s32[]{:S(2)}) async-start(), calls=%async_computation.24 | async-start | bytes 163840
  682.6 90.0 %reduce-scatter.26.cloned.1.call-start = ((), (), s32[]{:S(2)}) async-start(), calls=%async_computation.23 | async-start | bytes 3538944 | tf_op jit(solution)/shard_map/reduce_scatter | solution.py:312
  689.1 123.6 %reduce-scatter.20.cloned.1.call-start = ((), (), s32[]{:S(2)}) async-start(), calls=%async_computation.20 | async-start | bytes 1327104 | tf_op jit(solution)/shard_map/reduce_scatter | solution.py:303
  692.9 160.0 %reduce-scatter.22.cloned.1.call-start = ((), (), s32[]{:S(2)}) async-start(), calls=%async_computation.21 | async-start | bytes 1327104 | tf_op jit(solution)/shard_map/reduce_scatter | solution.py:306
  695.1 195.8 %reduce-scatter.16.cloned.1.call-start = ((), (), s32[]{:S(2)}) async-start(), calls=%async_computation.18 | async-start | bytes 1966080 | tf_op jit(solution)/shard_map/reduce_scatter | solution.py:281
  695.7 245.7 %reduce-scatter.18.cloned.1.call-start = ((), (), s32[]{:S(2)}) async-start(), calls=%async_computation.19 | async-start | bytes 3981312 | tf_op jit(solution)/shard_map/reduce_scatter | solution.py:297
  701.9 304.4 %reduce-scatter.24.cloned.1.call-start = ((), (), s32[]{:S(2)}) async-start(), calls=%async_computation.22 | async-start | bytes 7077888 | tf_op jit(solution)/shard_map/reduce_scatter | solution.py:309
  (70 other events, 223.7 us)
Sparse Core Ops, SparseCore 0:
  9.6 39.7 all-gather.7
  51.3 32.8 all-gather.9
  86.1 24.0 all-gather.11
  111.9 24.0 all-gather.13
  163.8 120.9 all-reduce.4
  287.1 44.5 all-gather.15
  333.3 37.0 all-gather.17
  387.0 119.9 all-reduce.6
  509.3 34.2 reduce-scatter.13
  667.2 35.1 reduce-scatter.29
  705.2 19.1 reduce-scatter.27
  728.0 44.5 reduce-scatter.25
  775.9 36.7 reduce-scatter.19
  816.1 36.7 reduce-scatter.21
  855.6 35.2 reduce-scatter.15
  894.3 47.0 reduce-scatter.17
  944.6 61.7 reduce-scatter.23
